TPU v7x, 32 devices: a whole 2x2x4 slice. The times are simulated.
32 devices in a mesh: size: 4 (over z), gz: 8 (over y, x, core).
Axes of the slice: x: 2, y: 2, z: 4, core: 2. Of those that a mesh axis runs over, the one named last changes fastest.
Arguments:
- tissue: int32 [256, 64, 128], P('gz'), may hold values from 0 to 2
- vessel_pressure: float32 [256, 64, 128], P('gz', 'size'), may hold values from -12 to 12
- cond_table: float32 [3], replicated, may hold values from 0.4 to 1.2
- leak_table: float32 [3], replicated, may hold values from 0.2 to 2
- bind_table: float32 [4, 3], P('size'), may hold values from 0.05 to 1
- hindrance: float32 [4], P('size'), may hold values from 0.2 to 1
- diffusivity: float32 [4], P('size'), may hold values from 0.1 to 0.6
- free_conc: float32 [4, 256, 64, 128], P('size', 'gz'), may hold values from 0 to 2
- bound_conc: float32 [4, 256, 64, 128], P('size', 'gz'), may hold values from 0 to 1
Outputs:
- pressure: float32 [256, 64, 128], P('gz', 'size')
- free_out: float32 [4, 256, 64, 128], P('size', 'gz')
- bound_out: float32 [4, 256, 64, 128], P('size', 'gz')
Inputs may be any that keep to these rules, and one draw needn't show every extreme that they name: 0 marks a vessel cell, 1 necrotic tissue, 2 viable tissue.
All inputs are finite; a program needn't handle non-finite values.
Results may differ from a plain program's by a relative error of at most 0.0001.
Values sent between devices are 32-bit elements; how exact they have to be, the bound alone decides.
No kernel may reach another device: no remote copies, remote signals or barrier semaphores. Data moves between devices by JAX's collectives and lax.ppermute only.
A program may use at most 128 MiB of HBM per device.

v0:
```python
import jax
import jax.numpy as jnp
from jax import lax
from jax.sharding import PartitionSpec as P

ITERS = 2
TSTEPS = 2
time_step = 0.1


def extended(cells, sides, width):
    for axis, dim in sides:
        count = lax.axis_size(axis)
        ends = count - 1
        head = lax.slice_in_dim(cells, 0, width, axis=dim)
        tail = lax.slice_in_dim(cells, cells.shape[dim] - width, cells.shape[dim], axis=dim)
        cells = jnp.concatenate(
            [
                lax.ppermute(tail, axis, [(i, (i + 1) % count) for i in range(ends)]),
                cells,
                lax.ppermute(head, axis, [((i + 1) % count, i) for i in range(ends)]),
            ],
            axis=dim,
        )
    return cells


def lookup(table, labels):
    return jnp.where(labels == 0, table[0], jnp.where(labels == 1, table[1], table[2]))


def neighbours(padded):
    total = padded[2:, 1:-1, 1:-1] + padded[:-2, 1:-1, 1:-1]
    total = total + padded[1:-1, 2:, 1:-1] + padded[1:-1, :-2, 1:-1]
    total = total + padded[1:-1, 1:-1, 2:] + padded[1:-1, 1:-1, :-2]
    return total


def apply_operator(vector, conduct, leak):
    scaled = conduct * vector
    rimmed = extended(scaled, (("size", 1), ("gz", 0)), 1)
    padded = jnp.pad(rimmed, ((0, 0), (0, 0), (1, 1)))
    return conduct * (6.0 * scaled - neighbours(padded)) + leak * vector


def paired_products(residual, precond, image):
    return lax.psum((jnp.sum(residual * precond), jnp.sum(precond * image)), ("size", "gz"))


def along_line(array, along_dim):
    return array[tuple((slice(None) if k == along_dim else slice(1, -1) for k in range(3)))]


def lower_part(array, along_dim):
    return array[tuple((slice(0, -1) if k == along_dim else slice(None) for k in range(3)))]


def upper_part(array, along_dim):
    return array[tuple((slice(1, None) if k == along_dim else slice(None) for k in range(3)))]


def transport_step(conc_pad, fields_pad, hinder, diffuse):
    divergence = None
    for along_dim in range(3):
        conc_line = along_line(conc_pad, along_dim)
        press_line = along_line(fields_pad[0], along_dim)
        cond_line = along_line(fields_pad[1], along_dim)
        conc_low = lower_part(conc_line, along_dim)
        conc_high = upper_part(conc_line, along_dim)
        velocity = (
            hinder
            * lower_part(cond_line, along_dim)
            * upper_part(cond_line, along_dim)
            * (lower_part(press_line, along_dim) - upper_part(press_line, along_dim))
        )
        flux = (
            jnp.maximum(velocity, 0.0) * conc_low
            + jnp.minimum(velocity, 0.0) * conc_high
            + diffuse * (conc_low - conc_high)
        )
        term = upper_part(flux, along_dim) - lower_part(flux, along_dim)
        divergence = term if divergence is None else divergence + term
    conc = conc_pad[1:-1, 1:-1, 1:-1]
    rate = fields_pad[2][1:-1, 1:-1, 1:-1]
    bind = rate * conc
    return (conc - time_step * (divergence + bind), bind)


def pad_plane(array):
    return jnp.pad(array, ((0, 0), (1, 1), (1, 1)))


def local(
    tissue,
    vessel_pressure,
    cond_table,
    leak_table,
    bind_table,
    hindrance,
    diffusivity,
    free_conc,
    bound_conc,
):
    block_x = vessel_pressure.shape[1]
    slab_z = vessel_pressure.shape[0]
    local_tissue = lax.dynamic_slice_in_dim(tissue, lax.axis_index("size") * block_x, block_x, 1)
    conduct = lookup(cond_table, local_tissue)
    leak = lookup(leak_table, local_tissue)
    diag = 6.0 * conduct * conduct + leak
    source = leak * vessel_pressure
    solution = jnp.zeros_like(source)
    residual = source
    precond = residual / diag
    image = apply_operator(precond, conduct, leak)
    rho_now, product = paired_products(residual, precond, image)
    alpha = rho_now / product
    direction = precond
    along_image = image
    for iteration in range(ITERS):
        solution = solution + alpha * direction
        residual = residual - alpha * along_image
        if iteration + 1 < ITERS:
            precond = residual / diag
            image = apply_operator(precond, conduct, leak)
            rho_next, product = paired_products(residual, precond, image)
            ratio = rho_next / rho_now
            alpha = rho_next / (product - ratio * rho_next / alpha)
            direction = precond + ratio * direction
            along_image = image + ratio * along_image
            rho_now = rho_next
    conduct_slab = lookup(cond_table, tissue)
    rate_slab = lookup(bind_table[0], tissue)
    slab_pressure = lax.all_gather(solution, "size", axis=1, tiled=True)
    stacked = jnp.stack([slab_pressure, conduct_slab, rate_slab])
    rimmed = extended(stacked, (("gz", 1),), TSTEPS)
    fields_pad = jnp.pad(rimmed, ((0, 0), (0, 0), (1, 1), (1, 1)))
    hinder = hindrance[0]
    diffuse = diffusivity[0]
    conc = free_conc[0]
    bound = bound_conc[0]
    fields_one = fields_pad[:, TSTEPS - 1 : TSTEPS + 1 + slab_z]
    for sweep in range(TSTEPS):
        conc_pad = pad_plane(extended(conc, (("gz", 0),), 1))
        conc, bind = transport_step(conc_pad, fields_one, hinder, diffuse)
        bound = bound + time_step * bind
    return (solution, conc[None], bound[None])


def solution(mesh):
    return jax.shard_map(
        local,
        mesh=mesh,
        in_specs=(
            P("gz", None, None),
            P("gz", "size", None),
            P(),
            P(),
            P("size", None),
            P("size"),
            P("size"),
            P("size", "gz", None, None),
            P("size", "gz", None, None),
        ),
        out_specs=(P("gz", "size", None), P("size", "gz", None, None), P("size", "gz", None, None)),
        check_vma=False,
    )
```

profile of v0, /device:TPU:4, one launch (start us, length us, event | category | flops | bytes accessed | tf_op | source)
XLA Modules:
  0.0 228.2 jit_solution(11120340233154857061)
XLA Ops:
  10.0 4.9 %fusion.39 = (f32[32,16,128]{2,1,0:T(8,128)S(1)}, pred[32,16,128]{2,1,0:T(8,128)(4,1)S(1)}, pred[32,16,128]{2,1,0:T(8,128)(4,1)S(1)}) fusion(f32[]{:T(128)} %bitcast.5, f32[]{:T(128)} %bitcast.4, f32[]{:T(128)} %bitcast.3, f32[32,16,128]{2,1,0:T(8,128)} %param.10, f32[]{:T(128)} %bitcast.2, f32[]{:T(128)} %bitcast.1, f32[]{:T(128)} %bitcast, ...), kind=kLoop, calls=%fused_computation.127 | loop fusion | flops 786432 | bytes 917532 | tf_op jit(solution)/shard_map/mul | solution.py:40
  16.3 4.5 %collective-permute-start = (f32[32,1,128]{2,1,0:T(1,128)S(1)}, f32[32,1,128]{2,1,0:T(1,128)S(1)}, u32[]{:S(2)}, u32[]{:S(2)}) collective-permute-start(f32[32,1,128]{2,1,0:T(1,128)S(1)} %get-tuple-element.41), channel_id=1, source_target_pairs={{0,8},{8,16},{16,24},{1,9},{9,17},{17,25},{2,10},{10,18},{18,26},{... | collective-permute-start | bytes 49160 | tf_op jit(solution)/shard_map/ppermute | solution.py:19
  24.2 2.4 %collective-permute-start.3 = (f32[1,18,128]{2,1,0:T(8,128)S(1)}, f32[1,18,128]{2,1,0:T(8,128)S(1)}, u32[]{:S(2)}, u32[]{:S(2)}) collective-permute-start(f32[1,18,128]{2,1,0:T(8,128)S(1)} %get-tuple-element.37), channel_id=1, source_target_pairs={{0,1},{1,2},{2,3},{3,4},{4,5},{5,6},{6,7},{8,9},{9,10},{10,11},{11... | collective-permute-start | bytes 27656 | tf_op jit(solution)/shard_map/ppermute | solution.py:19
  26.6 3.5 %collective-permute-done.3 = f32[1,18,128]{2,1,0:T(8,128)S(1)} collective-permute-done((f32[1,18,128]{2,1,0:T(8,128)S(1)}, f32[1,18,128]{2,1,0:T(8,128)S(1)}, u32[]{:S(2)}, u32[]{:S(2)}) %collective-permute-start.3) | collective-permute-done | bytes 9248 | tf_op jit(solution)/shard_map/ppermute | solution.py:19
  30.5 4.7 %multiply_reduce_fusion.1 = (f32[]{:T(128)}, f32[]{:T(128)}, f32[32,16,128]{2,1,0:T(8,128)S(1)}) fusion(pred[32,16,128]{2,1,0:T(8,128)(4,1)S(1)} %get-tuple-element.23, pred[32,16,128]{2,1,0:T(8,128)(4,1)S(1)} %get-tuple-element.22, f32[]{:T(128)} %bitcast.5, f32[]{:T(128)} %bitcast.4, f32[]{:T(128)} %bitcast.3, f32[32,16,128]{2,1,0:T(8,128)S(1)} %copy-done.1, ...), kind=kLoop, calls=%fused_computation.123 | loop fusion | flops 2031614 | bytes 1493024 | tf_op jit(solution)/shard_map/reduce_sum | solution.py:47
  35.3 41.6 %all-reduce.6 = (f32[]{:T(128)}, f32[]{:T(128)}) all-reduce(f32[]{:T(128)} %get-tuple-element.4, f32[]{:T(128)} %get-tuple-element.3), channel_id=1, replica_groups=mesh['size'=4,'gz'=8] {'size','gz'}, use_global_device_ids=true, to_apply=%region_1.2 | all-reduce | flops 2 | bytes 16 | tf_op jit(solution)/shard_map/psum | solution.py:47
  78.1 4.5 %fusion.38 = (f32[32,16,128]{2,1,0:T(8,128)S(1)}, f32[]{:T(128)}) fusion(pred[32,16,128]{2,1,0:T(8,128)(4,1)S(1)} %get-tuple-element.23, pred[32,16,128]{2,1,0:T(8,128)(4,1)S(1)} %get-tuple-element.22, f32[]{:T(128)} %bitcast.5, f32[]{:T(128)} %bitcast.4, f32[]{:T(128)} %bitcast.3, f32[32,16,128]{2,1,0:T(8,128)S(1)} %get-tuple-element.20, f32[]{:T(128)S(6)} %div.19, ...), kind=kLoop, calls=%fused_computation.126 | loop fusion | flops 917503 | bytes 917536 | tf_op jit(solution)/shard_map/mul | solution.py:40
  84.2 4.7 %collective-permute-start.4 = (f32[32,1,128]{2,1,0:T(1,128)S(1)}, f32[32,1,128]{2,1,0:T(1,128)S(1)}, u32[]{:S(2)}, u32[]{:S(2)}) collective-permute-start(f32[32,1,128]{2,1,0:T(1,128)S(1)} %get-tuple-element.39), channel_id=1, source_target_pairs={{0,8},{8,16},{16,24},{1,9},{9,17},{17,25},{2,10},{10,18},{18,26},{... | collective-permute-start | bytes 49160 | tf_op jit(solution)/shard_map/ppermute | solution.py:19
  92.2 2.4 %collective-permute-start.7 = (f32[1,18,128]{2,1,0:T(8,128)S(1)}, f32[1,18,128]{2,1,0:T(8,128)S(1)}, u32[]{:S(2)}, u32[]{:S(2)}) collective-permute-start(f32[1,18,128]{2,1,0:T(8,128)S(1)} %get-tuple-element.35), channel_id=1, source_target_pairs={{0,1},{1,2},{2,3},{3,4},{4,5},{5,6},{6,7},{8,9},{9,10},{10,11},{11... | collective-permute-start | bytes 27656 | tf_op jit(solution)/shard_map/ppermute | solution.py:19
  94.6 3.5 %collective-permute-done.7 = f32[1,18,128]{2,1,0:T(8,128)S(1)} collective-permute-done((f32[1,18,128]{2,1,0:T(8,128)S(1)}, f32[1,18,128]{2,1,0:T(8,128)S(1)}, u32[]{:S(2)}, u32[]{:S(2)}) %collective-permute-start.7) | collective-permute-done | bytes 9248 | tf_op jit(solution)/shard_map/ppermute | solution.py:19
  98.5 4.8 %fusion.28 = f32[]{:T(128)} fusion(f32[34,18,130]{2,1,0:T(8,128)S(1)} %select_maximum_fusion.8, f32[32,16,128]{2,1,0:T(8,128)S(1)} %get-tuple-element.33, f32[32,1,128]{2,1,0:T(1,128)S(1)} %collective-permute-done.4, f32[32,1,128]{2,1,0:T(1,128)S(1)} %collective-permute-done.5, f32[1,18,128]{2,1,0:T(8,128)S(1)} %collective-permute-done.7, ...), kind=kLoop, calls=%fused_computation.91 | loop fusion | flops 2031615 | bytes 1493024 | tf_op jit(solution)/shard_map/reduce_sum | solution.py:47
  103.3 41.4 %all-reduce.5 = (f32[]{:T(128)}, f32[]{:T(128)}) all-reduce(f32[]{:T(128)} %get-tuple-element.34, f32[]{:T(128)} %fusion.28), channel_id=1, replica_groups=mesh['size'=4,'gz'=8] {'size','gz'}, use_global_device_ids=true, to_apply=%region_5.6 | all-reduce | flops 2 | bytes 16 | tf_op jit(solution)/shard_map/psum | solution.py:47
  149.1 4.6 %multiply_add_fusion.6 = f32[32,16,128]{2,1,0:T(8,128)} fusion(f32[]{:T(128)S(6)} %div.21, f32[]{:T(128)S(6)} %div.23, f32[]{:T(128)S(6)} %div.19, pred[32,16,128]{2,1,0:T(8,128)(4,1)S(1)} %get-tuple-element.23, pred[32,16,128]{2,1,0:T(8,128)(4,1)S(1)} %get-tuple-element.22, f32[]{:T(128)} %bitcast.5, f32[]{:T(128)} %bitcast.4, f32[]{:T(128)} %bitcast.3, ...), kind=kLoop, calls=%fused_computation.120 | loop fusion | flops 1114112 | bytes 917540 | tf_op jit(solution)/shard_map/add | solution.py:120
  155.7 2.3 %collective-permute-start.10 = (f32[1,64,128]{2,1,0:T(8,128)S(1)}, f32[1,64,128]{2,1,0:T(8,128)S(1)}, u32[]{:S(2)}, u32[]{:S(2)}) collective-permute-start(f32[1,64,128]{2,1,0:T(8,128)S(1)} %get-tuple-element.31), channel_id=1, source_target_pairs={{0,1},{1,2},{2,3},{3,4},{4,5},{5,6},{6,7},{8,9},{9,10},{10,11},{11... | collective-permute-start | bytes 98312 | tf_op jit(solution)/shard_map/ppermute | solution.py:19
  160.0 2.2 select_bitcast_fusion.1
  164.3 17.5 %all-gather.2.cloned.1.call-done = f32[32,64,128]{2,1,0:T(8,128)} async-done(((f32[32,16,128]{2,1,0:T(8,128)}), f32[32,64,128]{2,1,0:T(8,128)}) %all-gather.2.cloned.1.call-update) | async-done | bytes 1048592 | tf_op jit(solution)/shard_map/all_gather | solution.py:133
  182.7 2.4 %collective-permute-start.9 = (f32[3,2,64,128]{3,2,1,0:T(8,128)S(1)}, f32[3,2,64,128]{3,2,1,0:T(8,128)S(1)}, u32[]{:S(2)}, u32[]{:S(2)}) collective-permute-start(f32[3,2,64,128]{3,2,1,0:T(8,128)S(1)} %get-tuple-element.28), channel_id=1, source_target_pairs={{1,0},{2,1},{3,2},{4,3},{5,4},{6,5},{7,6},{9,8},{10,9},{11,10},{12... | collective-permute-start | bytes 589832 | tf_op jit(solution)/shard_map/ppermute | solution.py:21
  185.1 2.2 collective-permute-start.8
  188.2 4.7 %collective-permute-done.8 = f32[3,2,64,128]{3,2,1,0:T(8,128)S(1)} collective-permute-done((f32[3,2,64,128]{3,2,1,0:T(8,128)S(1)}, f32[3,2,64,128]{3,2,1,0:T(8,128)S(1)}, u32[]{:S(2)}, u32[]{:S(2)}) %collective-permute-start.8) | collective-permute-done | bytes 196640 | tf_op jit(solution)/shard_map/ppermute | solution.py:19
  193.0 7.3 %select_maximum_fusion = f32[3,36,66,130]{3,2,1,0:T(8,128)S(1)} fusion(f32[3,2,64,128]{3,2,1,0:T(8,128)S(1)} %collective-permute-done.9, f32[3,2,64,128]{3,2,1,0:T(8,128)S(1)} %collective-permute-done.8, f32[1,32,64,128]{3,2,1,0:T(8,128)S(1)} %select_bitcast_fusion, f32[1,32,64,128]{3,2,1,0:T(8,128)S(1)} %get-tuple-element.17, f32[1,32,64,128]{3,2,1,0:T(8,128)S(1)} %bitcast.52), kind=kLoop, calls=%fused_computation.4 | loop fusion | flops 19459440 | bytes 7245504 | tf_op jit(solution)/shard_map/concatenate | solution.py:17
  200.9 2.4 %multiply_add_fusion.1 = (f32[32,64,129]{2,1,0:T(8,128)S(1)}, f32[32,64,129]{2,1,0:T(8,128)S(1)}) fusion(f32[34,66,130]{2,1,0:T(8,128)S(1)} %select_maximum_fusion.6, f32[]{:T(128)} %bitcast.45, f32[34,66,130]{2,1,0:T(8,128)S(1)} %get-tuple-element.25, f32[34,66,130]{2,1,0:T(8,128)S(1)} %get-tuple-element.24, f32[]{:T(128)} %bitcast.42), kind=kLoop, calls=%fused_computation.30 | loop fusion | flops 3170304 | bytes 8454152 | tf_op jit(solution)/shard_map/add | solution.py:77
  206.5 2.1 fusion.21
  210.4 2.6 %collective-permute-start.12 = (f32[1,64,128]{2,1,0:T(8,128)S(1)}, f32[1,64,128]{2,1,0:T(8,128)S(1)}, u32[]{:S(2)}, u32[]{:S(2)}) collective-permute-start(f32[1,64,128]{2,1,0:T(8,128)S(1)} %get-tuple-element.29), channel_id=1, source_target_pairs={{0,1},{1,2},{2,3},{3,4},{4,5},{5,6},{6,7},{8,9},{9,10},{10,11},{11... | collective-permute-start | bytes 98312 | tf_op jit(solution)/shard_map/ppermute | solution.py:19
  213.1 3.5 %collective-permute-done.12 = f32[1,64,128]{2,1,0:T(8,128)S(1)} collective-permute-done((f32[1,64,128]{2,1,0:T(8,128)S(1)}, f32[1,64,128]{2,1,0:T(8,128)S(1)}, u32[]{:S(2)}, u32[]{:S(2)}) %collective-permute-start.12) | collective-permute-done | bytes 32800 | tf_op jit(solution)/shard_map/ppermute | solution.py:19
  (60 shorter events, 30.1 us)
Async XLA Ops:
  7.2 23.3 %copy-start.1 = (f32[32,16,128]{2,1,0:T(8,128)S(1)}, f32[32,16,128]{2,1,0:T(8,128)}, u32[]{:S(2)}) copy-start(f32[32,16,128]{2,1,0:T(8,128)} %param.10) | copy-start | bytes 786436
  7.2 174.6 %all-gather.2.cloned.1.call-start = ((), (), s32[]{:S(2)}) async-start(), calls=%async_computation | async-start | bytes 1310720 | tf_op jit(solution)/shard_map/all_gather | solution.py:133
  15.0 5.9 %collective-permute-start.1 = (f32[32,1,128]{2,1,0:T(1,128)S(1)}, f32[32,1,128]{2,1,0:T(1,128)S(1)}, u32[]{:S(2)}, u32[]{:S(2)}) collective-permute-start(f32[32,1,128]{2,1,0:T(1,128)S(1)} %get-tuple-element.42), channel_id=1, source_target_pairs={{8,0},{16,8},{24,16},{9,1},{17,9},{25,17},{10,2},{18,10},{26,18},{... | collective-permute-start | bytes 49160 | tf_op jit(solution)/shard_map/ppermute | solution.py:21
  16.3 6.0 %collective-permute-start = (f32[32,1,128]{2,1,0:T(1,128)S(1)}, f32[32,1,128]{2,1,0:T(1,128)S(1)}, u32[]{:S(2)}, u32[]{:S(2)}) collective-permute-start(f32[32,1,128]{2,1,0:T(1,128)S(1)} %get-tuple-element.41), channel_id=1, source_target_pairs={{0,8},{8,16},{16,24},{1,9},{9,17},{17,25},{2,10},{10,18},{18,26},{... | collective-permute-start | bytes 49160 | tf_op jit(solution)/shard_map/ppermute | solution.py:19
  22.2 4.3 %collective-permute-start.2 = (f32[1,18,128]{2,1,0:T(8,128)S(1)}, f32[1,18,128]{2,1,0:T(8,128)S(1)}, u32[]{:S(2)}, u32[]{:S(2)}) collective-permute-start(f32[1,18,128]{2,1,0:T(8,128)S(1)} %get-tuple-element.38), channel_id=1, source_target_pairs={{1,0},{2,1},{3,2},{4,3},{5,4},{6,5},{7,6},{9,8},{10,9},{11,10},{12... | collective-permute-start | bytes 27656 | tf_op jit(solution)/shard_map/ppermute | solution.py:21
  24.2 5.9 %collective-permute-start.3 = (f32[1,18,128]{2,1,0:T(8,128)S(1)}, f32[1,18,128]{2,1,0:T(8,128)S(1)}, u32[]{:S(2)}, u32[]{:S(2)}) collective-permute-start(f32[1,18,128]{2,1,0:T(8,128)S(1)} %get-tuple-element.37), channel_id=1, source_target_pairs={{0,1},{1,2},{2,3},{3,4},{4,5},{5,6},{6,7},{8,9},{9,10},{10,11},{11... | collective-permute-start | bytes 27656 | tf_op jit(solution)/shard_map/ppermute | solution.py:19
  82.7 71.0 %copy-start = (f32[1,32,64,128]{3,2,1,0:T(8,128)S(1)}, f32[1,32,64,128]{3,2,1,0:T(8,128)}, u32[]{:S(2)}) copy-start(f32[1,32,64,128]{3,2,1,0:T(8,128)} %param.16) | copy-start | bytes 3145732
  82.7 6.1 %collective-permute-start.5 = (f32[32,1,128]{2,1,0:T(1,128)S(1)}, f32[32,1,128]{2,1,0:T(1,128)S(1)}, u32[]{:S(2)}, u32[]{:S(2)}) collective-permute-start(f32[32,1,128]{2,1,0:T(1,128)S(1)} %get-tuple-element.40), channel_id=1, source_target_pairs={{8,0},{16,8},{24,16},{9,1},{17,9},{25,17},{10,2},{18,10},{26,18},{... | collective-permute-start | bytes 49160 | tf_op jit(solution)/shard_map/ppermute | solution.py:21
  84.1 75.2 %copy-start.9 = (f32[1,3]{1,0:T(1,128)S(1)}, f32[1,3]{1,0:T(1,128)}, u32[]{:S(2)}) copy-start(f32[1,3]{1,0:T(1,128)} %param.13) | copy-start | bytes 40
  84.1 75.9 %copy-start.3 = (s32[32,64,128]{2,1,0:T(8,128)S(1)}, s32[32,64,128]{2,1,0:T(8,128)}, u32[]{:S(2)}) copy-start(s32[32,64,128]{2,1,0:T(8,128)} %param.9) | copy-start | bytes 3145732
  84.2 6.1 %collective-permute-start.4 = (f32[32,1,128]{2,1,0:T(1,128)S(1)}, f32[32,1,128]{2,1,0:T(1,128)S(1)}, u32[]{:S(2)}, u32[]{:S(2)}) collective-permute-start(f32[32,1,128]{2,1,0:T(1,128)S(1)} %get-tuple-element.39), channel_id=1, source_target_pairs={{0,8},{8,16},{16,24},{1,9},{9,17},{17,25},{2,10},{10,18},{18,26},{... | collective-permute-start | bytes 49160 | tf_op jit(solution)/shard_map/ppermute | solution.py:19
  90.3 4.3 %collective-permute-start.6 = (f32[1,18,128]{2,1,0:T(8,128)S(1)}, f32[1,18,128]{2,1,0:T(8,128)S(1)}, u32[]{:S(2)}, u32[]{:S(2)}) collective-permute-start(f32[1,18,128]{2,1,0:T(8,128)S(1)} %get-tuple-element.36), channel_id=1, source_target_pairs={{1,0},{2,1},{3,2},{4,3},{5,4},{6,5},{7,6},{9,8},{10,9},{11,10},{12... | collective-permute-start | bytes 27656 | tf_op jit(solution)/shard_map/ppermute | solution.py:21
  92.2 5.9 %collective-permute-start.7 = (f32[1,18,128]{2,1,0:T(8,128)S(1)}, f32[1,18,128]{2,1,0:T(8,128)S(1)}, u32[]{:S(2)}, u32[]{:S(2)}) collective-permute-start(f32[1,18,128]{2,1,0:T(8,128)S(1)} %get-tuple-element.35), channel_id=1, source_target_pairs={{0,1},{1,2},{2,3},{3,4},{4,5},{5,6},{6,7},{8,9},{9,10},{10,11},{11... | collective-permute-start | bytes 27656 | tf_op jit(solution)/shard_map/ppermute | solution.py:19
  153.7 33.6 %collective-permute-start.11 = (f32[1,64,128]{2,1,0:T(8,128)S(1)}, f32[1,64,128]{2,1,0:T(8,128)S(1)}, u32[]{:S(2)}, u32[]{:S(2)}) collective-permute-start(f32[1,64,128]{2,1,0:T(8,128)S(1)} %get-tuple-element.32), channel_id=1, source_target_pairs={{1,0},{2,1},{3,2},{4,3},{5,4},{6,5},{7,6},{9,8},{10,9},{11,10},{12... | collective-permute-start | bytes 98312 | tf_op jit(solution)/shard_map/ppermute | solution.py:21
  155.7 31.6 %collective-permute-start.10 = (f32[1,64,128]{2,1,0:T(8,128)S(1)}, f32[1,64,128]{2,1,0:T(8,128)S(1)}, u32[]{:S(2)}, u32[]{:S(2)}) collective-permute-start(f32[1,64,128]{2,1,0:T(8,128)S(1)} %get-tuple-element.31), channel_id=1, source_target_pairs={{0,1},{1,2},{2,3},{3,4},{4,5},{5,6},{6,7},{8,9},{9,10},{10,11},{11... | collective-permute-start | bytes 98312 | tf_op jit(solution)/shard_map/ppermute | solution.py:19
  182.6 10.3 %copy-start.2 = (f32[32,64,128]{2,1,0:T(8,128)S(1)}, f32[32,64,128]{2,1,0:T(8,128)}, u32[]{:S(2)}) copy-start(f32[32,64,128]{2,1,0:T(8,128)} %all-gather.2.cloned.1.call-done) | copy-start | bytes 3145732
  182.7 5.6 %collective-permute-start.9 = (f32[3,2,64,128]{3,2,1,0:T(8,128)S(1)}, f32[3,2,64,128]{3,2,1,0:T(8,128)S(1)}, u32[]{:S(2)}, u32[]{:S(2)}) collective-permute-start(f32[3,2,64,128]{3,2,1,0:T(8,128)S(1)} %get-tuple-element.28), channel_id=1, source_target_pairs={{1,0},{2,1},{3,2},{4,3},{5,4},{6,5},{7,6},{9,8},{10,9},{11,10},{12... | collective-permute-start | bytes 589832 | tf_op jit(solution)/shard_map/ppermute | solution.py:21
  185.1 7.9 %collective-permute-start.8 = (f32[3,2,64,128]{3,2,1,0:T(8,128)S(1)}, f32[3,2,64,128]{3,2,1,0:T(8,128)S(1)}, u32[]{:S(2)}, u32[]{:S(2)}) collective-permute-start(f32[3,2,64,128]{3,2,1,0:T(8,128)S(1)} %get-tuple-element.27), channel_id=1, source_target_pairs={{0,1},{1,2},{2,3},{3,4},{4,5},{5,6},{6,7},{8,9},{9,10},{10,11},{11... | collective-permute-start | bytes 589832 | tf_op jit(solution)/shard_map/ppermute | solution.py:19
  187.3 5.6 %copy-start.5 = (f32[1,64,128]{2,1,0:T(8,128)}, f32[1,64,128]{2,1,0:T(8,128)S(1)}, u32[]{:S(2)}) copy-start(f32[1,64,128]{2,1,0:T(8,128)S(1)} %collective-permute-done.11) | copy-start | bytes 98308
  187.3 5.6 %copy-start.7 = (f32[1,64,128]{2,1,0:T(8,128)}, f32[1,64,128]{2,1,0:T(8,128)S(1)}, u32[]{:S(2)}) copy-start(f32[1,64,128]{2,1,0:T(8,128)S(1)} %collective-permute-done.10) | copy-start | bytes 98308
  203.3 1.9 copy-start.6
  203.3 1.9 copy-start.8
  208.5 4.6 %collective-permute-start.13 = (f32[1,64,128]{2,1,0:T(8,128)S(1)}, f32[1,64,128]{2,1,0:T(8,128)S(1)}, u32[]{:S(2)}, u32[]{:S(2)}) collective-permute-start(f32[1,64,128]{2,1,0:T(8,128)S(1)} %get-tuple-element.30), channel_id=1, source_target_pairs={{1,0},{2,1},{3,2},{4,3},{5,4},{6,5},{7,6},{9,8},{10,9},{11,10},{12... | collective-permute-start | bytes 98312 | tf_op jit(solution)/shard_map/ppermute | solution.py:21
  210.4 6.1 %collective-permute-start.12 = (f32[1,64,128]{2,1,0:T(8,128)S(1)}, f32[1,64,128]{2,1,0:T(8,128)S(1)}, u32[]{:S(2)}, u32[]{:S(2)}) collective-permute-start(f32[1,64,128]{2,1,0:T(8,128)S(1)} %get-tuple-element.29), channel_id=1, source_target_pairs={{0,1},{1,2},{2,3},{3,4},{4,5},{5,6},{6,7},{8,9},{9,10},{10,11},{11... | collective-permute-start | bytes 98312 | tf_op jit(solution)/shard_map/ppermute | solution.py:19
  (1 other events, 1.2 us)
Sparse Core Ops, SparseCore 0:
  153.8 27.8 all-gather.1
where the time goes:
time: 229 us; the launch traced here: 228 us
  blocking collectives  83 us (36%)
  other arithmetic  49.8 us (22%)
  waiting for transfers between devices  35.7 us (16%)
  starting transfers between devices  34.1 us (15%)
  between operations  21.4 us (9%)
  local copies, waits for them, and re-layouts  4.21 us (2%)
    psum x2, blocking collectives, paired_products(): lax.psum((jnp.sum(residual * precond), jnp.sum(precond * image)), ('size'...  83 us
    ppermute x7, starting transfers between devices, extended(): lax.ppermute(tail, axis, [(i, (i + 1) % count) for i in range(ends)])  21.2 us
    ppermute x7, waiting for transfers between devices, extended(): lax.ppermute(tail, axis, [(i, (i + 1) % count) for i in range(ends)])  18 us
    all_gather x1, waiting for transfers between devices, local(): slab_pressure = lax.all_gather(solution, 'size', axis=1, tiled=True)  17.5 us
    ppermute x7, starting transfers between devices, extended(): lax.ppermute(head, axis, [((i + 1) % count, i) for i in range(ends)])  12.8 us
    concatenate x7, other arithmetic, extended(): jnp.concatenate([lax.ppermute(tail, axis, [(i, (i + 1) % count) for i in...  9.57 us
    reduce_sum x2, other arithmetic, paired_products(): jnp.sum(precond * image)  9.51 us
    mul x2, other arithmetic, apply_operator(): scaled = conduct * vector  9.43 us
  transfers between devices with their start and end apart: 15, of which 8 were waited for; matrix products, arithmetic and copies ran while one was open for 3% of the time, Pallas kernels for 0%

commit v1 on v0

--- a/solution.py
+++ b/solution.py
@@ -6,6 +6,21 @@
 ITERS = 2
 TSTEPS = 2
 time_step = 0.1
+
+
+def _take_column(state):
+    degree = lax.axis_size("size")
+    windows = [state]
+    q = 0
+    while q < degree - 1:
+        windows.append(
+            lax.ppermute(windows[-1], "size", [(c, (c + 1) % degree) for c in range(degree)])
+        )
+        q = q + 1
+    passed = jnp.roll(
+        jnp.concatenate(windows[::-1], axis=1), (lax.axis_index("size") + 1) * state.shape[1], 1
+    )
+    return passed
 
 
 def extended(cells, sides, width):
@@ -130,7 +145,7 @@
             rho_now = rho_next
     conduct_slab = lookup(cond_table, tissue)
     rate_slab = lookup(bind_table[0], tissue)
-    slab_pressure = lax.all_gather(solution, "size", axis=1, tiled=True)
+    slab_pressure = _take_column(solution)
     stacked = jnp.stack([slab_pressure, conduct_slab, rate_slab])
     rimmed = extended(stacked, (("gz", 1),), TSTEPS)
     fields_pad = jnp.pad(rimmed, ((0, 0), (0, 0), (1, 1), (1, 1)))

time: 229 us -> 215 us (0.939)
  between operations: 21.4 us -> 8.08 us
    all_gather x1 -> x0, waiting for transfers between devices: 17.5 us -> none  [local(): slab_pressure = lax.all_gather(solution, 'size', axis=1, tiled=True)]
    ppermute x0 -> x3, waiting for transfers between devices: none -> 15.8 us  [_take_column(): lax.ppermute(windows[-1], 'size', [(c, (c + 1) % degree) for c in range(d...]
  transfers between devices with their start and end apart: 15 -> 17, of which waited for: 8 -> 10; matrix products, arithmetic and copies ran while one was open for 3% -> 3% of each run, Pallas kernels for 0% -> 0%
where the time goes in v1:
time: 215 us; the launch traced here: 214 us
  blocking collectives  83 us (39%)
  other arithmetic  49 us (23%)
  starting transfers between devices  35.3 us (16%)
  waiting for transfers between devices  34 us (16%)
  between operations  8.08 us (4%)
  local copies, waits for them, and re-layouts  4.47 us (2%)
    psum x2, blocking collectives, paired_products(): lax.psum((jnp.sum(residual * precond), jnp.sum(precond * image)), ('size'...  83 us
    ppermute x7, starting transfers between devices, extended(): lax.ppermute(tail, axis, [(i, (i + 1) % count) for i in range(ends)])  21.2 us
    ppermute x7, waiting for transfers between devices, extended(): lax.ppermute(tail, axis, [(i, (i + 1) % count) for i in range(ends)])  17.3 us
    ppermute x3, waiting for transfers between devices, _take_column(): lax.ppermute(windows[-1], 'size', [(c, (c + 1) % degree) for c in range(d...  15.8 us
    ppermute x7, starting transfers between devices, extended(): lax.ppermute(head, axis, [((i + 1) % count, i) for i in range(ends)])  12.6 us
    reduce_sum x2, other arithmetic, paired_products(): jnp.sum(precond * image)  9.7 us
    mul x2, other arithmetic, apply_operator(): scaled = conduct * vector  9.7 us
    concatenate x7, other arithmetic, extended(): jnp.concatenate([lax.ppermute(tail, axis, [(i, (i + 1) % count) for i in...  9.55 us
  transfers between devices with their start and end apart: 17, of which 10 were waited for; matrix products, arithmetic and copies ran while one was open for 3% of the time, Pallas kernels for 0%

profile of v1, /device:TPU:4, one launch (start us, length us, event | category | flops | bytes accessed | tf_op | source)
XLA Modules:
  0.0 213.8 jit_solution(10435729309855684228)
XLA Ops:
  3.5 5.0 %fusion.39 = (f32[32,16,128]{2,1,0:T(8,128)S(1)}, pred[32,16,128]{2,1,0:T(8,128)(4,1)S(1)}, pred[32,16,128]{2,1,0:T(8,128)(4,1)S(1)}) fusion(f32[]{:T(128)} %bitcast.5, f32[]{:T(128)} %bitcast.4, f32[]{:T(128)} %bitcast.3, f32[32,16,128]{2,1,0:T(8,128)} %param.10, f32[]{:T(128)} %bitcast.2, f32[]{:T(128)} %bitcast.1, f32[]{:T(128)} %bitcast, ...), kind=kLoop, calls=%fused_computation.128 | loop fusion | flops 786432 | bytes 917532 | tf_op jit(solution)/shard_map/mul | solution.py:55
  9.9 4.5 %collective-permute-start = (f32[32,1,128]{2,1,0:T(1,128)S(1)}, f32[32,1,128]{2,1,0:T(1,128)S(1)}, u32[]{:S(2)}, u32[]{:S(2)}) collective-permute-start(f32[32,1,128]{2,1,0:T(1,128)S(1)} %get-tuple-element.41), channel_id=1, source_target_pairs={{0,8},{8,16},{16,24},{1,9},{9,17},{17,25},{2,10},{10,18},{18,26},{... | collective-permute-start | bytes 49160 | tf_op jit(solution)/shard_map/ppermute | solution.py:34
  17.8 2.4 %collective-permute-start.3 = (f32[1,18,128]{2,1,0:T(8,128)S(1)}, f32[1,18,128]{2,1,0:T(8,128)S(1)}, u32[]{:S(2)}, u32[]{:S(2)}) collective-permute-start(f32[1,18,128]{2,1,0:T(8,128)S(1)} %get-tuple-element.37), channel_id=1, source_target_pairs={{0,1},{1,2},{2,3},{3,4},{4,5},{5,6},{6,7},{8,9},{9,10},{10,11},{11... | collective-permute-start | bytes 27656 | tf_op jit(solution)/shard_map/ppermute | solution.py:34
  20.2 3.5 %collective-permute-done.3 = f32[1,18,128]{2,1,0:T(8,128)S(1)} collective-permute-done((f32[1,18,128]{2,1,0:T(8,128)S(1)}, f32[1,18,128]{2,1,0:T(8,128)S(1)}, u32[]{:S(2)}, u32[]{:S(2)}) %collective-permute-start.3) | collective-permute-done | bytes 9248 | tf_op jit(solution)/shard_map/ppermute | solution.py:34
  24.1 4.9 %multiply_reduce_fusion.1 = (f32[]{:T(128)}, f32[]{:T(128)}, f32[32,16,128]{2,1,0:T(8,128)S(1)}) fusion(pred[32,16,128]{2,1,0:T(8,128)(4,1)S(1)} %get-tuple-element.23, pred[32,16,128]{2,1,0:T(8,128)(4,1)S(1)} %get-tuple-element.22, f32[]{:T(128)} %bitcast.5, f32[]{:T(128)} %bitcast.4, f32[]{:T(128)} %bitcast.3, f32[32,16,128]{2,1,0:T(8,128)S(1)} %copy-done.1, ...), kind=kLoop, calls=%fused_computation.124 | loop fusion | flops 2031614 | bytes 1493024 | tf_op jit(solution)/shard_map/reduce_sum | solution.py:62
  29.0 41.5 %all-reduce.6 = (f32[]{:T(128)}, f32[]{:T(128)}) all-reduce(f32[]{:T(128)} %get-tuple-element.4, f32[]{:T(128)} %get-tuple-element.3), channel_id=1, replica_groups=mesh['size'=4,'gz'=8] {'size','gz'}, use_global_device_ids=true, to_apply=%region_1.2 | all-reduce | flops 2 | bytes 16 | tf_op jit(solution)/shard_map/psum | solution.py:62
  71.8 4.7 %fusion.38 = (f32[32,16,128]{2,1,0:T(8,128)S(1)}, f32[]{:T(128)}) fusion(pred[32,16,128]{2,1,0:T(8,128)(4,1)S(1)} %get-tuple-element.23, pred[32,16,128]{2,1,0:T(8,128)(4,1)S(1)} %get-tuple-element.22, f32[]{:T(128)} %bitcast.5, f32[]{:T(128)} %bitcast.4, f32[]{:T(128)} %bitcast.3, f32[32,16,128]{2,1,0:T(8,128)S(1)} %get-tuple-element.20, f32[]{:T(128)S(6)} %div.19, ...), kind=kLoop, calls=%fused_computation.127 | loop fusion | flops 917503 | bytes 917536 | tf_op jit(solution)/shard_map/mul | solution.py:55
  77.9 4.5 %collective-permute-start.4 = (f32[32,1,128]{2,1,0:T(1,128)S(1)}, f32[32,1,128]{2,1,0:T(1,128)S(1)}, u32[]{:S(2)}, u32[]{:S(2)}) collective-permute-start(f32[32,1,128]{2,1,0:T(1,128)S(1)} %get-tuple-element.39), channel_id=1, source_target_pairs={{0,8},{8,16},{16,24},{1,9},{9,17},{17,25},{2,10},{10,18},{18,26},{... | collective-permute-start | bytes 49160 | tf_op jit(solution)/shard_map/ppermute | solution.py:34
  85.8 2.4 %collective-permute-start.7 = (f32[1,18,128]{2,1,0:T(8,128)S(1)}, f32[1,18,128]{2,1,0:T(8,128)S(1)}, u32[]{:S(2)}, u32[]{:S(2)}) collective-permute-start(f32[1,18,128]{2,1,0:T(8,128)S(1)} %get-tuple-element.35), channel_id=1, source_target_pairs={{0,1},{1,2},{2,3},{3,4},{4,5},{5,6},{6,7},{8,9},{9,10},{10,11},{11... | collective-permute-start | bytes 27656 | tf_op jit(solution)/shard_map/ppermute | solution.py:34
  88.2 3.5 %collective-permute-done.7 = f32[1,18,128]{2,1,0:T(8,128)S(1)} collective-permute-done((f32[1,18,128]{2,1,0:T(8,128)S(1)}, f32[1,18,128]{2,1,0:T(8,128)S(1)}, u32[]{:S(2)}, u32[]{:S(2)}) %collective-permute-start.7) | collective-permute-done | bytes 9248 | tf_op jit(solution)/shard_map/ppermute | solution.py:34
  92.1 4.8 %fusion.28 = f32[]{:T(128)} fusion(f32[34,18,130]{2,1,0:T(8,128)S(1)} %select_maximum_fusion.8, f32[32,16,128]{2,1,0:T(8,128)S(1)} %get-tuple-element.33, f32[32,1,128]{2,1,0:T(1,128)S(1)} %collective-permute-done.4, f32[32,1,128]{2,1,0:T(1,128)S(1)} %collective-permute-done.5, f32[1,18,128]{2,1,0:T(8,128)S(1)} %collective-permute-done.7, ...), kind=kLoop, calls=%fused_computation.92 | loop fusion | flops 2031615 | bytes 1493024 | tf_op jit(solution)/shard_map/reduce_sum | solution.py:62
  97.0 41.4 %all-reduce.5 = (f32[]{:T(128)}, f32[]{:T(128)}) all-reduce(f32[]{:T(128)} %get-tuple-element.34, f32[]{:T(128)} %fusion.28), channel_id=1, replica_groups=mesh['size'=4,'gz'=8] {'size','gz'}, use_global_device_ids=true, to_apply=%region_5.6 | all-reduce | flops 2 | bytes 16 | tf_op jit(solution)/shard_map/psum | solution.py:62
  142.8 4.0 %multiply_add_fusion.6 = f32[32,16,128]{2,1,0:T(8,128)S(1)} fusion(f32[]{:T(128)S(6)} %div.21, f32[]{:T(128)S(6)} %div.23, f32[]{:T(128)S(6)} %div.19, pred[32,16,128]{2,1,0:T(8,128)(4,1)S(1)} %get-tuple-element.23, pred[32,16,128]{2,1,0:T(8,128)(4,1)S(1)} %get-tuple-element.22, f32[]{:T(128)} %bitcast.5, f32[]{:T(128)} %bitcast.4, f32[]{:T(128)} %bitcast.3, ...), kind=kLoop, calls=%fused_computation.121 | loop fusion | flops 1114112 | bytes 917540 | tf_op jit(solution)/shard_map/add | solution.py:135
  148.3 7.6 %collective-permute-done.8 = f32[32,16,128]{2,1,0:T(8,128)S(1)} collective-permute-done((f32[32,16,128]{2,1,0:T(8,128)S(1)}, f32[32,16,128]{2,1,0:T(8,128)S(1)}, u32[]{:S(2)}, u32[]{:S(2)}) %collective-permute-start.8) | collective-permute-done | bytes 262176 | tf_op jit(solution)/shard_map/ppermute | solution.py:17
  157.9 2.4 %collective-permute-start.13 = (f32[1,64,128]{2,1,0:T(8,128)S(1)}, f32[1,64,128]{2,1,0:T(8,128)S(1)}, u32[]{:S(2)}, u32[]{:S(2)}) collective-permute-start(f32[1,64,128]{2,1,0:T(8,128)S(1)} %get-tuple-element.31), channel_id=1, source_target_pairs={{0,1},{1,2},{2,3},{3,4},{4,5},{5,6},{6,7},{8,9},{9,10},{10,11},{11... | collective-permute-start | bytes 98312 | tf_op jit(solution)/shard_map/ppermute | solution.py:34
  164.1 2.3 %select_bitcast_fusion.1 = (f32[1,32,64,128]{3,2,1,0:T(8,128)S(1)}, pred[32,64,128]{2,1,0:T(8,128)(4,1)S(1)}, pred[32,64,128]{2,1,0:T(8,128)(4,1)S(1)}) fusion(f32[]{:T(128)} %bitcast.5, f32[]{:T(128)} %bitcast.4, f32[]{:T(128)} %bitcast.3, s32[32,64,128]{2,1,0:T(8,128)S(1)} %copy-done.3), kind=kLoop, calls=%fused_computation.70 | loop fusion | flops 1048576 | bytes 2621452 | tf_op jit(solution)/shard_map/stack | solution.py:149
  166.5 6.3 %collective-permute-done.10 = f32[32,16,128]{2,1,0:T(8,128)S(1)} collective-permute-done((f32[32,16,128]{2,1,0:T(8,128)S(1)}, f32[32,16,128]{2,1,0:T(8,128)S(1)}, u32[]{:S(2)}, u32[]{:S(2)}) %collective-permute-start.10) | collective-permute-done | bytes 262176 | tf_op jit(solution)/shard_map/ppermute | solution.py:17
  175.2 2.3 %collective-permute-start.12 = (f32[3,2,64,128]{3,2,1,0:T(8,128)S(1)}, f32[3,2,64,128]{3,2,1,0:T(8,128)S(1)}, u32[]{:S(2)}, u32[]{:S(2)}) collective-permute-start(f32[3,2,64,128]{3,2,1,0:T(8,128)S(1)} %get-tuple-element.28), channel_id=1, source_target_pairs={{1,0},{2,1},{3,2},{4,3},{5,4},{6,5},{7,6},{9,8},{10,9},{11,10},{12... | collective-permute-start | bytes 589832 | tf_op jit(solution)/shard_map/ppermute | solution.py:36
  177.5 2.2 %collective-permute-start.11 = (f32[3,2,64,128]{3,2,1,0:T(8,128)S(1)}, f32[3,2,64,128]{3,2,1,0:T(8,128)S(1)}, u32[]{:S(2)}, u32[]{:S(2)}) collective-permute-start(f32[3,2,64,128]{3,2,1,0:T(8,128)S(1)} %get-tuple-element.27), channel_id=1, source_target_pairs={{0,1},{1,2},{2,3},{3,4},{4,5},{5,6},{6,7},{8,9},{9,10},{10,11},{11... | collective-permute-start | bytes 589832 | tf_op jit(solution)/shard_map/ppermute | solution.py:34
  181.4 4.0 %collective-permute-done.11 = f32[3,2,64,128]{3,2,1,0:T(8,128)S(1)} collective-permute-done((f32[3,2,64,128]{3,2,1,0:T(8,128)S(1)}, f32[3,2,64,128]{3,2,1,0:T(8,128)S(1)}, u32[]{:S(2)}, u32[]{:S(2)}) %collective-permute-start.11) | collective-permute-done | bytes 196640 | tf_op jit(solution)/shard_map/ppermute | solution.py:34
  185.4 7.2 %select_maximum_fusion = f32[3,36,66,130]{3,2,1,0:T(8,128)S(1)} fusion(f32[3,2,64,128]{3,2,1,0:T(8,128)S(1)} %collective-permute-done.12, f32[3,2,64,128]{3,2,1,0:T(8,128)S(1)} %collective-permute-done.11, f32[1,32,64,128]{3,2,1,0:T(8,128)S(1)} %get-tuple-element.52, f32[1,32,64,128]{3,2,1,0:T(8,128)S(1)} %get-tuple-element.17, ...), kind=kLoop, calls=%fused_computation.4 | loop fusion | flops 19459440 | bytes 7245504 | tf_op jit(solution)/shard_map/concatenate | solution.py:32
  193.3 2.4 %multiply_add_fusion.1 = (f32[32,64,129]{2,1,0:T(8,128)S(1)}, f32[32,64,129]{2,1,0:T(8,128)S(1)}) fusion(f32[34,66,130]{2,1,0:T(8,128)S(1)} %select_maximum_fusion.6, f32[]{:T(128)} %bitcast.46, f32[34,66,130]{2,1,0:T(8,128)S(1)} %get-tuple-element.25, f32[34,66,130]{2,1,0:T(8,128)S(1)} %get-tuple-element.24, f32[]{:T(128)} %bitcast.43), kind=kLoop, calls=%fused_computation.30 | loop fusion | flops 3170304 | bytes 8454152 | tf_op jit(solution)/shard_map/add | solution.py:92
  202.8 2.6 %collective-permute-start.15 = (f32[1,64,128]{2,1,0:T(8,128)S(1)}, f32[1,64,128]{2,1,0:T(8,128)S(1)}, u32[]{:S(2)}, u32[]{:S(2)}) collective-permute-start(f32[1,64,128]{2,1,0:T(8,128)S(1)} %get-tuple-element.29), channel_id=1, source_target_pairs={{0,1},{1,2},{2,3},{3,4},{4,5},{5,6},{6,7},{8,9},{9,10},{10,11},{11... | collective-permute-start | bytes 98312 | tf_op jit(solution)/shard_map/ppermute | solution.py:34
  205.5 3.5 %collective-permute-done.15 = f32[1,64,128]{2,1,0:T(8,128)S(1)} collective-permute-done((f32[1,64,128]{2,1,0:T(8,128)S(1)}, f32[1,64,128]{2,1,0:T(8,128)S(1)}, u32[]{:S(2)}, u32[]{:S(2)}) %collective-permute-start.15) | collective-permute-done | bytes 32800 | tf_op jit(solution)/shard_map/ppermute | solution.py:34
  (71 shorter events, 35.5 us)
Async XLA Ops:
  0.6 23.5 %copy-start.1 = (f32[32,16,128]{2,1,0:T(8,128)S(1)}, f32[32,16,128]{2,1,0:T(8,128)}, u32[]{:S(2)}) copy-start(f32[32,16,128]{2,1,0:T(8,128)} %param.10) | copy-start | bytes 786436
  8.6 5.9 %collective-permute-start.1 = (f32[32,1,128]{2,1,0:T(1,128)S(1)}, f32[32,1,128]{2,1,0:T(1,128)S(1)}, u32[]{:S(2)}, u32[]{:S(2)}) collective-permute-start(f32[32,1,128]{2,1,0:T(1,128)S(1)} %get-tuple-element.42), channel_id=1, source_target_pairs={{8,0},{16,8},{24,16},{9,1},{17,9},{25,17},{10,2},{18,10},{26,18},{... | collective-permute-start | bytes 49160 | tf_op jit(solution)/shard_map/ppermute | solution.py:36
  9.9 6.0 %collective-permute-start = (f32[32,1,128]{2,1,0:T(1,128)S(1)}, f32[32,1,128]{2,1,0:T(1,128)S(1)}, u32[]{:S(2)}, u32[]{:S(2)}) collective-permute-start(f32[32,1,128]{2,1,0:T(1,128)S(1)} %get-tuple-element.41), channel_id=1, source_target_pairs={{0,8},{8,16},{16,24},{1,9},{9,17},{17,25},{2,10},{10,18},{18,26},{... | collective-permute-start | bytes 49160 | tf_op jit(solution)/shard_map/ppermute | solution.py:34
  15.9 4.3 %collective-permute-start.2 = (f32[1,18,128]{2,1,0:T(8,128)S(1)}, f32[1,18,128]{2,1,0:T(8,128)S(1)}, u32[]{:S(2)}, u32[]{:S(2)}) collective-permute-start(f32[1,18,128]{2,1,0:T(8,128)S(1)} %get-tuple-element.38), channel_id=1, source_target_pairs={{1,0},{2,1},{3,2},{4,3},{5,4},{6,5},{7,6},{9,8},{10,9},{11,10},{12... | collective-permute-start | bytes 27656 | tf_op jit(solution)/shard_map/ppermute | solution.py:36
  17.8 5.9 %collective-permute-start.3 = (f32[1,18,128]{2,1,0:T(8,128)S(1)}, f32[1,18,128]{2,1,0:T(8,128)S(1)}, u32[]{:S(2)}, u32[]{:S(2)}) collective-permute-start(f32[1,18,128]{2,1,0:T(8,128)S(1)} %get-tuple-element.37), channel_id=1, source_target_pairs={{0,1},{1,2},{2,3},{3,4},{4,5},{5,6},{6,7},{8,9},{9,10},{10,11},{11... | collective-permute-start | bytes 27656 | tf_op jit(solution)/shard_map/ppermute | solution.py:34
  76.4 79.5 %copy-start = (f32[1,32,64,128]{3,2,1,0:T(8,128)S(1)}, f32[1,32,64,128]{3,2,1,0:T(8,128)}, u32[]{:S(2)}) copy-start(f32[1,32,64,128]{3,2,1,0:T(8,128)} %param.16) | copy-start | bytes 3145732
  76.4 85.2 %copy-start.9 = (f32[1,3]{1,0:T(1,128)S(1)}, f32[1,3]{1,0:T(1,128)}, u32[]{:S(2)}) copy-start(f32[1,3]{1,0:T(1,128)} %param.13) | copy-start | bytes 40
  76.4 87.7 %copy-start.3 = (s32[32,64,128]{2,1,0:T(8,128)S(1)}, s32[32,64,128]{2,1,0:T(8,128)}, u32[]{:S(2)}) copy-start(s32[32,64,128]{2,1,0:T(8,128)} %param.9) | copy-start | bytes 3145732
  76.5 6.0 %collective-permute-start.5 = (f32[32,1,128]{2,1,0:T(1,128)S(1)}, f32[32,1,128]{2,1,0:T(1,128)S(1)}, u32[]{:S(2)}, u32[]{:S(2)}) collective-permute-start(f32[32,1,128]{2,1,0:T(1,128)S(1)} %get-tuple-element.40), channel_id=1, source_target_pairs={{8,0},{16,8},{24,16},{9,1},{17,9},{25,17},{10,2},{18,10},{26,18},{... | collective-permute-start | bytes 49160 | tf_op jit(solution)/shard_map/ppermute | solution.py:36
  77.9 6.0 %collective-permute-start.4 = (f32[32,1,128]{2,1,0:T(1,128)S(1)}, f32[32,1,128]{2,1,0:T(1,128)S(1)}, u32[]{:S(2)}, u32[]{:S(2)}) collective-permute-start(f32[32,1,128]{2,1,0:T(1,128)S(1)} %get-tuple-element.39), channel_id=1, source_target_pairs={{0,8},{8,16},{16,24},{1,9},{9,17},{17,25},{2,10},{10,18},{18,26},{... | collective-permute-start | bytes 49160 | tf_op jit(solution)/shard_map/ppermute | solution.py:34
  83.9 4.3 %collective-permute-start.6 = (f32[1,18,128]{2,1,0:T(8,128)S(1)}, f32[1,18,128]{2,1,0:T(8,128)S(1)}, u32[]{:S(2)}, u32[]{:S(2)}) collective-permute-start(f32[1,18,128]{2,1,0:T(8,128)S(1)} %get-tuple-element.36), channel_id=1, source_target_pairs={{1,0},{2,1},{3,2},{4,3},{5,4},{6,5},{7,6},{9,8},{10,9},{11,10},{12... | collective-permute-start | bytes 27656 | tf_op jit(solution)/shard_map/ppermute | solution.py:36
  85.8 5.9 %collective-permute-start.7 = (f32[1,18,128]{2,1,0:T(8,128)S(1)}, f32[1,18,128]{2,1,0:T(8,128)S(1)}, u32[]{:S(2)}, u32[]{:S(2)}) collective-permute-start(f32[1,18,128]{2,1,0:T(8,128)S(1)} %get-tuple-element.35), channel_id=1, source_target_pairs={{0,1},{1,2},{2,3},{3,4},{4,5},{5,6},{6,7},{8,9},{9,10},{10,11},{11... | collective-permute-start | bytes 27656 | tf_op jit(solution)/shard_map/ppermute | solution.py:34
  146.9 26.2 %copy-start.2 = (f32[32,16,128]{2,1,0:T(8,128)}, f32[32,16,128]{2,1,0:T(8,128)S(1)}, u32[]{:S(2)}) copy-start(f32[32,16,128]{2,1,0:T(8,128)S(1)} %multiply_add_fusion.6) | copy-start | bytes 786436
  146.9 9.1 %collective-permute-start.8 = (f32[32,16,128]{2,1,0:T(8,128)S(1)}, f32[32,16,128]{2,1,0:T(8,128)S(1)}, u32[]{:S(2)}, u32[]{:S(2)}) collective-permute-start(f32[32,16,128]{2,1,0:T(8,128)S(1)} %multiply_add_fusion.6), channel_id=1, source_target_pairs={{0,8},{8,16},{16,24},{24,0},{1,9},{9,17},{17,25},{25,1},{2,10},{10... | collective-permute-start | bytes 786440 | tf_op jit(solution)/shard_map/ppermute | solution.py:17
  156.0 8.2 %collective-permute-start.9 = (f32[32,16,128]{2,1,0:T(8,128)S(1)}, f32[32,16,128]{2,1,0:T(8,128)S(1)}, u32[]{:S(2)}, u32[]{:S(2)}) collective-permute-start(f32[32,16,128]{2,1,0:T(8,128)S(1)} %collective-permute-done.8), channel_id=1, source_target_pairs={{0,8},{8,16},{16,24},{24,0},{1,9},{9,17},{17,25},{25,1},{2,10},{10... | collective-permute-start | bytes 786440 | tf_op jit(solution)/shard_map/ppermute | solution.py:17
  156.0 23.7 %collective-permute-start.14 = (f32[1,64,128]{2,1,0:T(8,128)S(1)}, f32[1,64,128]{2,1,0:T(8,128)S(1)}, u32[]{:S(2)}, u32[]{:S(2)}) collective-permute-start(f32[1,64,128]{2,1,0:T(8,128)S(1)} %get-tuple-element.32), channel_id=1, source_target_pairs={{1,0},{2,1},{3,2},{4,3},{5,4},{6,5},{7,6},{9,8},{10,9},{11,10},{12... | collective-permute-start | bytes 98312 | tf_op jit(solution)/shard_map/ppermute | solution.py:36
  157.9 21.8 %collective-permute-start.13 = (f32[1,64,128]{2,1,0:T(8,128)S(1)}, f32[1,64,128]{2,1,0:T(8,128)S(1)}, u32[]{:S(2)}, u32[]{:S(2)}) collective-permute-start(f32[1,64,128]{2,1,0:T(8,128)S(1)} %get-tuple-element.31), channel_id=1, source_target_pairs={{0,1},{1,2},{2,3},{3,4},{4,5},{5,6},{6,7},{8,9},{9,10},{10,11},{11... | collective-permute-start | bytes 98312 | tf_op jit(solution)/shard_map/ppermute | solution.py:34
  164.1 8.7 %collective-permute-start.10 = (f32[32,16,128]{2,1,0:T(8,128)S(1)}, f32[32,16,128]{2,1,0:T(8,128)S(1)}, u32[]{:S(2)}, u32[]{:S(2)}) collective-permute-start(f32[32,16,128]{2,1,0:T(8,128)S(1)} %collective-permute-done.9), channel_id=1, source_target_pairs={{0,8},{8,16},{16,24},{24,0},{1,9},{9,17},{17,25},{25,1},{2,10},{10... | collective-permute-start | bytes 786440 | tf_op jit(solution)/shard_map/ppermute | solution.py:17
  175.2 6.2 %collective-permute-start.12 = (f32[3,2,64,128]{3,2,1,0:T(8,128)S(1)}, f32[3,2,64,128]{3,2,1,0:T(8,128)S(1)}, u32[]{:S(2)}, u32[]{:S(2)}) collective-permute-start(f32[3,2,64,128]{3,2,1,0:T(8,128)S(1)} %get-tuple-element.28), channel_id=1, source_target_pairs={{1,0},{2,1},{3,2},{4,3},{5,4},{6,5},{7,6},{9,8},{10,9},{11,10},{12... | collective-permute-start | bytes 589832 | tf_op jit(solution)/shard_map/ppermute | solution.py:36
  177.5 7.9 %collective-permute-start.11 = (f32[3,2,64,128]{3,2,1,0:T(8,128)S(1)}, f32[3,2,64,128]{3,2,1,0:T(8,128)S(1)}, u32[]{:S(2)}, u32[]{:S(2)}) collective-permute-start(f32[3,2,64,128]{3,2,1,0:T(8,128)S(1)} %get-tuple-element.27), channel_id=1, source_target_pairs={{0,1},{1,2},{2,3},{3,4},{4,5},{5,6},{6,7},{8,9},{9,10},{10,11},{11... | collective-permute-start | bytes 589832 | tf_op jit(solution)/shard_map/ppermute | solution.py:34
  179.7 5.6 %copy-start.5 = (f32[1,64,128]{2,1,0:T(8,128)}, f32[1,64,128]{2,1,0:T(8,128)S(1)}, u32[]{:S(2)}) copy-start(f32[1,64,128]{2,1,0:T(8,128)S(1)} %collective-permute-done.14) | copy-start | bytes 98308
  179.8 5.6 %copy-start.7 = (f32[1,64,128]{2,1,0:T(8,128)}, f32[1,64,128]{2,1,0:T(8,128)S(1)}, u32[]{:S(2)}) copy-start(f32[1,64,128]{2,1,0:T(8,128)S(1)} %collective-permute-done.13) | copy-start | bytes 98308
  200.9 4.6 %collective-permute-start.16 = (f32[1,64,128]{2,1,0:T(8,128)S(1)}, f32[1,64,128]{2,1,0:T(8,128)S(1)}, u32[]{:S(2)}, u32[]{:S(2)}) collective-permute-start(f32[1,64,128]{2,1,0:T(8,128)S(1)} %get-tuple-element.30), channel_id=1, source_target_pairs={{1,0},{2,1},{3,2},{4,3},{5,4},{6,5},{7,6},{9,8},{10,9},{11,10},{12... | collective-permute-start | bytes 98312 | tf_op jit(solution)/shard_map/ppermute | solution.py:36
  202.8 6.1 %collective-permute-start.15 = (f32[1,64,128]{2,1,0:T(8,128)S(1)}, f32[1,64,128]{2,1,0:T(8,128)S(1)}, u32[]{:S(2)}, u32[]{:S(2)}) collective-permute-start(f32[1,64,128]{2,1,0:T(8,128)S(1)} %get-tuple-element.29), channel_id=1, source_target_pairs={{0,1},{1,2},{2,3},{3,4},{4,5},{5,6},{6,7},{8,9},{9,10},{10,11},{11... | collective-permute-start | bytes 98312 | tf_op jit(solution)/shard_map/ppermute | solution.py:34
  (3 other events, 5.1 us)
